TPU v7x, 256 devices: a whole 4x4x8 slice. The times are simulated.
256 devices in a mesh: row: 32 (over x, z), col: 8 (over y, core).
Axes of the slice: x: 4, y: 4, z: 8, core: 2. Of those that a mesh axis runs over, the one named last changes fastest.
Arguments:
- mom_a: float32 [1536, 12288], P('row', 'col'), may hold values from -6 to 6
- grad_a: float32 [1536, 12288], P('row', 'col'), may hold values from -6 to 6
- basis_a: float32 [512, 12288], P('row', 'col'), may hold values from -0.0546875 to 0.0546875
- mom_b: float32 [7168, 1536], P('row', 'col'), may hold values from -6 to 6
- grad_b: float32 [7168, 1536], P('row', 'col'), may hold values from -6 to 6
- basis_b: float32 [512, 1536], P('row', 'col'), may hold values from -0.15625 to 0.15625
Outputs:
- new_mom_a: float32 [1536, 12288], P('row', 'col')
- update_a: bfloat16 [1536, 12288], P('row', 'col')
- new_basis_a: float32 [512, 12288], P('row', 'col')
- new_mom_b: float32 [7168, 1536], P('row', 'col')
- update_b: bfloat16 [7168, 1536], P('row', 'col')
- new_basis_b: float32 [512, 1536], P('row', 'col')
All inputs are finite; a program needn't handle non-finite values.
Results may differ from a plain program's by a relative error of at most 0.0049.
Values sent between devices are 32-bit elements; how exact they have to be, the bound alone decides.
No kernel may reach another device: no remote copies, remote signals or barrier semaphores. Data moves between devices by JAX's collectives and lax.ppermute only.
A program may use at most 64 MiB of HBM per device.

v0:
```python
import math

import jax
import jax.numpy as jnp
from jax import lax
from jax.sharding import PartitionSpec as P

MU = 0.95
EPS = 1e-06


def sent_to_all(array, axis):
    size = lax.axis_size(axis)
    return lax.all_to_all(
        jnp.broadcast_to(array[None], (size, *array.shape)), axis, 0, 0, tiled=True
    )


def over_copies(array, axis):
    everything = sent_to_all(array, axis)
    return jnp.sum(everything, axis=0)


def split_up(array, dim, size):
    before, after = (array.shape[:dim], array.shape[dim + 1 :])
    return jnp.moveaxis(array.reshape(*before, size, -1, *after), dim, 0)


def summed_on_arrival(array, axis, dim):
    size = lax.axis_size(axis)
    parts = lax.all_to_all(split_up(array, dim, size), axis, 0, 0, tiled=True)
    return jnp.sum(parts, axis=0)


def in_one_piece(arrays, axis, dim, along):
    widths = [a.shape[along] for a in arrays]
    both = jnp.concatenate(arrays, axis=along)
    whole = lax.all_gather(both, axis, axis=dim, tiled=True)
    return tuple(jnp.split(whole, [sum(widths[:k]) for k in range(1, len(widths))], axis=along))


def together(arrays, axis):
    ends = [0]
    for a in arrays:
        ends.append(ends[-1] + a.size)
    so_far = lax.psum(jnp.concatenate([a.ravel() for a in arrays]), axis)
    return tuple((so_far[b:e].reshape(a.shape) for a, b, e in zip(arrays, ends, ends[1:])))


def project(buffer, basis):
    partial_proj = jnp.dot(
        buffer,
        lax.all_gather(basis, "row", axis=0, tiled=True).T,
        precision=lax.Precision.HIGHEST,
        preferred_element_type=jnp.float32,
    )
    return over_copies(partial_proj, "col")


def local_gram(proj):
    return jnp.dot(
        proj.T, proj, precision=lax.Precision.HIGHEST, preferred_element_type=jnp.float32
    )


def finish(buffer, proj, gram):
    highest = lax.Precision.HIGHEST
    lower = jnp.linalg.cholesky(gram)
    ortho = lax.linalg.triangular_solve(lower, proj, left_side=False, lower=True, transpose_a=True)
    rank = ortho.shape[1]
    share = summed_on_arrival(
        jnp.dot(ortho.T, buffer, precision=highest, preferred_element_type=jnp.float32), "row", 0
    )
    squares = over_copies(jnp.sum(share * share, axis=1, keepdims=True), "col")
    norms = jnp.sqrt(squares + EPS)
    own_basis = share / norms
    full_basis, full_norms = in_one_piece((own_basis, norms), "row", 0, 1)
    trans = full_basis * full_norms
    new_mom = buffer - (1.0 - MU) * jnp.dot(
        ortho, trans, precision=highest, preferred_element_type=jnp.float32
    )
    total_rows = buffer.shape[0] * lax.axis_size("row")
    total_cols = buffer.shape[1] * lax.axis_size("col")
    scale = math.sqrt(total_rows * total_cols / rank)
    update = (
        jnp.dot(ortho, full_basis, precision=highest, preferred_element_type=jnp.float32) * scale
    ).astype(jnp.bfloat16)
    return (new_mom, update, own_basis)


def shards(mom_a, grad_a, basis_a, mom_b, grad_b, basis_b):
    buffers = [MU * mom_a + grad_a, MU * mom_b + grad_b]
    projs = [project(buffers[0], basis_a), project(buffers[1], basis_b)]
    grams = together((local_gram(projs[0]), local_gram(projs[1])), "row")
    first = finish(buffers[0], projs[0], grams[0])
    second = finish(buffers[1], projs[1], grams[1])
    return (first[0], first[1], first[2], second[0], second[1], second[2])


def solution(mesh):
    return jax.shard_map(
        shards,
        mesh=mesh,
        in_specs=(
            P("row", "col"),
            P("row", "col"),
            P("row", "col"),
            P("row", "col"),
            P("row", "col"),
            P("row", "col"),
        ),
        out_specs=(
            P("row", "col"),
            P("row", "col"),
            P("row", "col"),
            P("row", "col"),
            P("row", "col"),
            P("row", "col"),
        ),
        check_vma=False,
    )
```

profile of v0, /device:TPU:2, one launch (start us, length us, event | category | flops | bytes accessed | tf_op | source)
XLA Modules:
  0.0 711.2 jit_solution(5581359570950233791)
XLA Ops:
  7.9 52.2 %all_gather.13 = f32[512,192]{1,0:T(8,128)S(1)} all-gather(f32[16,192]{1,0:T(8,128)} %param.12), channel_id=1, replica_groups=mesh['row'=32,'col'=8] {'row'}, dimensions={0}, use_global_device_ids=true | all-gather | bytes 405504 | tf_op jit(solution)/shard_map/all_gather | solution.py:53
  64.5 4.6 all-to-all-start.1
  69.1 23.3 %all-gather.3.cloned.1.call-done = f32[512,1536]{1,0:T(8,128)} async-done(((f32[16,1536]{1,0:T(8,128)}), f32[512,1536]{1,0:T(8,128)}) %all-gather.3.cloned.1.call-update) | async-done | bytes 3145744 | tf_op jit(solution)/shard_map/all_gather | solution.py:53
  92.4 4.9 fusion.95
  97.3 15.9 %all-to-all-done.1 = f32[8,224,512]{2,1,0:T(8,128)} async-done(((f32[8,224,512]{2,1,0:T(8,128)}), f32[8,224,512]{2,1,0:T(8,128)}, u32[]{:S(2)}, u32[]{:S(2)}) %all-to-all-start.1) | async-done | bytes 3670048 | tf_op jit(solution)/shard_map/all_to_all | solution.py:14
  121.8 9.0 %all-to-all-done = f32[8,48,512]{2,1,0:T(8,128)S(1)} async-done(((f32[8,48,512]{2,1,0:T(8,128)}), f32[8,48,512]{2,1,0:T(8,128)S(1)}, u32[]{:S(2)}, u32[]{:S(2)}) %all-to-all-start) | async-done | bytes 786464 | tf_op jit(solution)/shard_map/all_to_all | solution.py:14
  133.6 149.1 %all-reduce.3.cloned.1.call-done = f32[524288]{0:T(1024)} async-done(((f32[524288]{0:T(1024)}), f32[524288]{0:T(1024)}) %all-reduce.3.cloned.1.call-update) | async-done | bytes 2097168 | tf_op jit(solution)/shard_map/psum | solution.py:46
  286.1 11.7 %cholesky.286 = f32[128,128]{1,0:T(8,128)S(1)} custom-call(f32[128,128]{1,0:T(8,128)S(1)} %cholesky.426), custom_call_target="Cholesky" | custom-call | tf_op jit(solution)/shard_map/jit(cholesky)/cholesky | solution.py:68
  297.9 9.8 %custom-call.31 = f32[1,128,128]{1,2,0:T(8,128)S(1)} custom-call(f32[1,128,128]{2,1,0:T(8,128)S(1)} %get-tuple-element.64), custom_call_target="InvertDiagBlocksLowerTriangular" | custom-call | tf_op jit(solution)/shard_map/jit(cholesky)/cholesky | solution.py:68
  308.5 11.9 %cholesky.305 = f32[128,128]{1,0:T(8,128)S(1)} custom-call(f32[128,128]{1,0:T(8,128)S(1)} %cholesky.430), custom_call_target="Cholesky" | custom-call | tf_op jit(solution)/shard_map/jit(cholesky)/cholesky | solution.py:68
  320.4 9.8 %custom-call.32 = f32[1,128,128]{1,2,0:T(8,128)S(1)} custom-call(f32[1,128,128]{2,1,0:T(8,128)S(1)} %get-tuple-element.61), custom_call_target="InvertDiagBlocksLowerTriangular" | custom-call | tf_op jit(solution)/shard_map/jit(cholesky)/cholesky | solution.py:68
  330.9 11.7 %cholesky.326 = f32[128,128]{1,0:T(8,128)S(1)} custom-call(f32[128,128]{1,0:T(8,128)S(1)} %cholesky.435), custom_call_target="Cholesky" | custom-call | tf_op jit(solution)/shard_map/jit(cholesky)/cholesky | solution.py:68
  343.3 9.8 %custom-call.33 = f32[1,128,128]{1,2,0:T(8,128)S(1)} custom-call(f32[1,128,128]{2,1,0:T(8,128)S(1)} %get-tuple-element.58), custom_call_target="InvertDiagBlocksLowerTriangular" | custom-call | tf_op jit(solution)/shard_map/jit(cholesky)/cholesky | solution.py:68
  353.7 12.1 %cholesky.343 = f32[128,128]{1,0:T(8,128)S(1)} custom-call(f32[128,128]{1,0:T(8,128)S(1)} %convolution_subtract_fusion.8), custom_call_target="Cholesky" | custom-call | tf_op jit(solution)/shard_map/jit(cholesky)/cholesky | solution.py:68
  369.9 8.0 %while.2 = (s32[]{:T(128)}, f32[512,512]{1,0:T(8,128)S(1)}, s32[4,2]{0,1:T(2,128)S(1)}, f32[4,128,128]{2,1,0:T(8,128)S(1)}, s32[]{:T(128)}) while((s32[]{:T(128)}, f32[512,512]{1,0:T(8,128)S(1)}, s32[4,2]{0,1:T(2,128)S(1)}, f32[4,128,128]{2,1,0:T(8,128)S(1)}, s32[]{:T(128)}) %tuple.57), condition=%wide.while_cond, body=%wide.while_body.sunk | while | flops 2 | bytes 131181 | solution.py:69
  377.9 39.3 %custom-call.26 = f32[4,128,128]{1,2,0:T(8,128)S(1)} custom-call(f32[4,128,128]{2,1,0:T(8,128)S(1)} %get-tuple-element.14), custom_call_target="InvertDiagBlocksLowerTriangular" | custom-call | tf_op jit(solution)/shard_map/triangular_solve | solution.py:69
  418.9 5.3 fusion.81
  424.2 7.5 %all-to-all-start.2 = ((f32[32,16,1536]{2,1,0:T(8,128)}), f32[32,16,1536]{2,1,0:T(8,128)S(1)}, u32[]{:S(2)}, u32[]{:S(2)}) async-start(f32[32,16,1536]{2,1,0:T(8,128)} %bitcast.114), calls=%async_computation.2 | async-start | bytes 6291456 | tf_op jit(solution)/shard_map/all_to_all | solution.py:31
  440.0 12.5 %cholesky.358 = f32[128,128]{1,0:T(8,128)S(1)} custom-call(f32[128,128]{1,0:T(8,128)} %cholesky.439), custom_call_target="Cholesky" | custom-call | tf_op jit(solution)/shard_map/jit(cholesky)/cholesky | solution.py:68
  453.2 11.3 %custom-call.34 = f32[1,128,128]{1,2,0:T(8,128)} custom-call(f32[1,128,128]{2,1,0:T(8,128)} %get-tuple-element.54), custom_call_target="InvertDiagBlocksLowerTriangular" | custom-call | tf_op jit(solution)/shard_map/jit(cholesky)/cholesky | solution.py:68
  470.1 12.5 %cholesky.377 = f32[128,128]{1,0:T(8,128)S(1)} custom-call(f32[128,128]{1,0:T(8,128)} %cholesky.443), custom_call_target="Cholesky" | custom-call | tf_op jit(solution)/shard_map/jit(cholesky)/cholesky | solution.py:68
  483.3 10.8 %custom-call.35 = f32[1,128,128]{1,2,0:T(8,128)S(1)} custom-call(f32[1,128,128]{2,1,0:T(8,128)} %get-tuple-element.51), custom_call_target="InvertDiagBlocksLowerTriangular" | custom-call | tf_op jit(solution)/shard_map/jit(cholesky)/cholesky | solution.py:68
  498.7 12.5 %cholesky.398 = f32[128,128]{1,0:T(8,128)S(1)} custom-call(f32[128,128]{1,0:T(8,128)} %cholesky.448), custom_call_target="Cholesky" | custom-call | tf_op jit(solution)/shard_map/jit(cholesky)/cholesky | solution.py:68
  512.0 10.6 %custom-call.36 = f32[1,128,128]{1,2,0:T(8,128)S(1)} custom-call(f32[1,128,128]{2,1,0:T(8,128)} %get-tuple-element.48), custom_call_target="InvertDiagBlocksLowerTriangular" | custom-call | tf_op jit(solution)/shard_map/jit(cholesky)/cholesky | solution.py:68
  527.2 4.3 all-to-all-start.3
  532.6 12.5 %cholesky.415 = f32[128,128]{1,0:T(8,128)S(1)} custom-call(f32[128,128]{1,0:T(8,128)} %convolution_subtract_fusion.7), custom_call_target="Cholesky" | custom-call | tf_op jit(solution)/shard_map/jit(cholesky)/cholesky | solution.py:68
  552.0 8.0 %while.3 = (s32[]{:T(128)}, f32[512,512]{1,0:T(8,128)S(1)}, s32[4,2]{0,1:T(2,128)S(1)}, f32[4,128,128]{2,1,0:T(8,128)S(1)}, s32[]{:T(128)}) while((s32[]{:T(128)}, f32[512,512]{1,0:T(8,128)S(1)}, s32[4,2]{0,1:T(2,128)S(1)}, f32[4,128,128]{2,1,0:T(8,128)S(1)}, s32[]{:T(128)}) %tuple.69), condition=%wide.while_cond.1, body=%wide.while_body.1.sunk | while | flops 2 | bytes 131181 | solution.py:69
  560.0 39.3 %custom-call.27 = f32[4,128,128]{1,2,0:T(8,128)S(1)} custom-call(f32[4,128,128]{2,1,0:T(8,128)S(1)} %get-tuple-element.22), custom_call_target="InvertDiagBlocksLowerTriangular" | custom-call | tf_op jit(solution)/shard_map/triangular_solve | solution.py:69
  602.5 30.6 %all_to_all.30 = f32[32,16,192]{2,1,0:T(8,128)S(1)} all-to-all(f32[32,16,192]{2,1,0:T(8,128)S(1)} %bitcast.117), channel_id=1, replica_groups=mesh['row'=32,'col'=8] {'row'}, dimensions={0} | all-to-all | bytes 786432 | tf_op jit(solution)/shard_map/all_to_all | solution.py:31
  633.3 10.0 %all_to_all.31 = f32[8,16,1]{1,2,0:T(1,128)S(1)} all-to-all(f32[8,16,1]{1,2,0:T(1,128)S(1)} %broadcast_in_dim.12), channel_id=1, replica_groups=mesh['row'=32,'col'=8] {'col'}, dimensions={0} | all-to-all | bytes 1024 | tf_op jit(solution)/shard_map/all_to_all | solution.py:14
  643.6 48.6 %all_gather.15 = f32[512,193]{1,0:T(8,128)S(1)} all-gather(f32[16,193]{1,0:T(8,128)S(1)} %pad_maximum_fusion.10), channel_id=1, replica_groups=mesh['row'=32,'col'=8] {'row'}, dimensions={0}, use_global_device_ids=true | all-gather | bytes 407616 | tf_op jit(solution)/shard_map/all_gather | solution.py:38
  695.9 4.7 fusion.14
  (169 shorter events, 82.9 us)
Async XLA Ops:
  7.2 85.2 %all-gather.3.cloned.1.call-start = ((), (), s32[]{:S(2)}) async-start(), calls=%async_computation.6 | async-start | bytes 3244032 | tf_op jit(solution)/shard_map/all_gather | solution.py:53
  64.5 27.9 %copy-start.4 = (f32[48,1536]{1,0:T(8,128)S(1)}, f32[48,1536]{1,0:T(8,128)}, u32[]{:S(2)}) copy-start(f32[48,1536]{1,0:T(8,128)} %param.8) | copy-start | bytes 884740
  64.5 27.9 %copy-start.5 = (f32[48,1536]{1,0:T(8,128)S(1)}, f32[48,1536]{1,0:T(8,128)}, u32[]{:S(2)}) copy-start(f32[48,1536]{1,0:T(8,128)} %param.7) | copy-start | bytes 884740
  64.5 48.7 %all-to-all-start.1 = ((f32[8,224,512]{2,1,0:T(8,128)}), f32[8,224,512]{2,1,0:T(8,128)}, u32[]{:S(2)}, u32[]{:S(2)}) async-start(f32[8,224,512]{2,1,0:T(8,128)} %broadcast_in_dim.10), calls=%async_computation.1 | async-start | bytes 7340032 | tf_op jit(solution)/shard_map/all_to_all | solution.py:14
  114.1 16.6 %all-to-all-start = ((f32[8,48,512]{2,1,0:T(8,128)}), f32[8,48,512]{2,1,0:T(8,128)S(1)}, u32[]{:S(2)}, u32[]{:S(2)}) async-start(f32[8,48,512]{2,1,0:T(8,128)} %broadcast_in_dim.8), calls=%async_computation | async-start | bytes 1572864 | tf_op jit(solution)/shard_map/all_to_all | solution.py:14
  117.7 165.0 %all-reduce.3.cloned.1.call-start = ((), (), s32[]{:S(2)}) async-start(), calls=%async_computation.7 | async-start | bytes 4194304 | tf_op jit(solution)/shard_map/psum | solution.py:46
  120.4 11.7 %copy-start.1 = (f32[224,512]{1,0:T(8,128)}, f32[224,512]{1,0:T(8,128)S(1)}, u32[]{:S(2)}) copy-start(f32[224,512]{1,0:T(8,128)S(1)} %reduce_sum.73) | copy-start | bytes 1376260
  417.4 6.7 copy-start.9
  417.9 6.3 copy-start.11
  418.3 5.9 copy-start.14
  418.9 5.3 copy-start.17
  424.2 102.1 %all-to-all-start.2 = ((f32[32,16,1536]{2,1,0:T(8,128)}), f32[32,16,1536]{2,1,0:T(8,128)S(1)}, u32[]{:S(2)}, u32[]{:S(2)}) async-start(f32[32,16,1536]{2,1,0:T(8,128)} %bitcast.114), calls=%async_computation.2 | async-start | bytes 6291456 | tf_op jit(solution)/shard_map/all_to_all | solution.py:31
  438.4 1.0 copy-start.3
  468.8 0.7 copy-start.13
  497.4 0.7 copy-start.16
  526.5 72.9 %copy-start.2 = (f32[224,512]{1,0:T(8,128)S(1)}, f32[224,512]{1,0:T(8,128)}, u32[]{:S(2)}) copy-start(f32[224,512]{1,0:T(8,128)} %copy-done.1) | copy-start | bytes 1376260
  527.2 19.2 %all-to-all-start.3 = ((f32[8,16,1]{1,2,0:T(1,128)}), f32[8,16,1]{1,2,0:T(1,128)S(1)}, u32[]{:S(2)}, u32[]{:S(2)}) async-start(f32[8,16,1]{1,2,0:T(1,128)} %broadcast_in_dim.11), calls=%async_computation.3 | async-start | bytes 8192 | tf_op jit(solution)/shard_map/all_to_all | solution.py:14
  531.5 164.3 %all-gather.5.cloned.1.call-start = ((), (), s32[]{:S(2)}) async-start(), calls=%async_computation.8 | async-start | bytes 3514368 | tf_op jit(solution)/shard_map/all_gather | solution.py:38
  546.6 54.6 %copy-start.19 = (f32[16,1536]{1,0:T(8,128)}, f32[16,1536]{1,0:T(8,128)S(1)}, u32[]{:S(2)}) copy-start(f32[16,1536]{1,0:T(8,128)S(1)} %broadcast_divide_fusion) | copy-start | bytes 294916
  547.4 54.1 %copy-start.7 = (f32[224,192]{0,1:T(8,128)S(1)}, f32[224,192]{0,1:T(8,128)}, u32[]{:S(2)}) copy-start(f32[224,192]{0,1:T(8,128)} %param.11) | copy-start | bytes 516100
  547.4 54.1 %copy-start.8 = (f32[224,192]{0,1:T(8,128)S(1)}, f32[224,192]{0,1:T(8,128)}, u32[]{:S(2)}) copy-start(f32[224,192]{0,1:T(8,128)} %param.10) | copy-start | bytes 516100
  601.5 94.4 %copy-start.10 = (f32[48,128]{1,0:T(8,128)S(1)}, f32[48,128]{1,0:T(8,128)}, u32[]{:S(2)}) copy-start(f32[48,128]{1,0:T(8,128)} %copy-done.9) | copy-start | bytes 73732
  601.5 94.3 %copy-start.12 = (f32[48,128]{1,0:T(8,128)S(1)}, f32[48,128]{1,0:T(8,128)}, u32[]{:S(2)}) copy-start(f32[48,128]{1,0:T(8,128)} %copy-done.11) | copy-start | bytes 73732
  601.5 94.3 %copy-start.15 = (f32[48,128]{1,0:T(8,128)S(1)}, f32[48,128]{1,0:T(8,128)}, u32[]{:S(2)}) copy-start(f32[48,128]{1,0:T(8,128)} %copy-done.14) | copy-start | bytes 73732
  601.5 94.3 %copy-start.18 = (f32[48,128]{1,0:T(8,128)S(1)}, f32[48,128]{1,0:T(8,128)}, u32[]{:S(2)}) copy-start(f32[48,128]{1,0:T(8,128)} %copy-done.17) | copy-start | bytes 73732
  643.5 57.0 %copy-start.20 = (f32[16,192]{1,0:T(8,128)}, f32[16,192]{1,0:T(8,128)S(1)}, u32[]{:S(2)}) copy-start(f32[16,192]{1,0:T(8,128)S(1)} %broadcast_divide_fusion.1) | copy-start | bytes 36868
  692.4 9.2 %copy-start.6 = (f32[48,1536]{1,0:T(8,128)S(1)}, f32[48,1536]{1,0:T(8,128)}, u32[]{:S(2)}) copy-start(f32[48,1536]{1,0:T(8,128)} %param.7) | copy-start | bytes 884740
  695.9 5.8 copy-start
Sparse Core Ops, SparseCore 0:
  10.6 81.7 all-gather.2
  133.7 148.9 all-reduce.2
  547.5 88.8 all-gather.4
where the time goes:
time: 717 us; the launch traced here: 711 us
  other arithmetic  254 us (35%)
  waiting for transfers between devices  198 us (28%)
  blocking collectives  141 us (20%)
  matrix products  42 us (6%)
  local copies, waits for them, and re-layouts  35.4 us (5%)
  starting transfers between devices  20.7 us (3%)
  between operations  19.8 us (3%)
    another operation x28, other arithmetic, finish(): lower = jnp.linalg.cholesky(gram)  166 us
    psum x1, waiting for transfers between devices, together(): so_far = lax.psum(jnp.concatenate([a.ravel() for a in arrays]), axis)  149 us
    another operation x5, other arithmetic, finish(): lax.linalg.triangular_solve(lower, proj, left_side=False, lower=True, tra...  80.1 us
    all_gather x1, blocking collectives, project(): lax.all_gather(basis, 'row', axis=0, tiled=True)  52.2 us
    all_gather x1, blocking collectives, in_one_piece(): whole = lax.all_gather(both, axis, axis=dim, tiled=True)  48.6 us
    all_to_all x1, blocking collectives, summed_on_arrival(): parts = lax.all_to_all(split_up(array, dim, size), axis, 0, 0, tiled=True)  30.6 us
    all_to_all x3, waiting for transfers between devices, sent_to_all(): lax.all_to_all(jnp.broadcast_to(array[None], (size, *array.shape)), axis,...  24.8 us
    all_gather x1, waiting for transfers between devices, project(): lax.all_gather(basis, 'row', axis=0, tiled=True)  23.3 us
  transfers between devices with their start and end apart: 7, of which 4 were waited for; matrix products, arithmetic and copies ran while one was open for 25% of the time, Pallas kernels for 0%

commit v1 on v0

v1 whole, which is shorter than its diff:
```python
import functools
import math

import jax
import jax.numpy as jnp
from jax import lax
from jax.experimental import pallas as pl
from jax.experimental.pallas import tpu as pltpu
from jax.sharding import Mesh
from jax.sharding import PartitionSpec as P

MU = 0.95
EPS = 1e-06
TILE = 128
STRIP = 16
HIGHEST = lax.Precision.HIGHEST


def contract(a, b, ca, cb):
    return lax.dot_general(
        a, b, (((ca,), (cb,)), ((), ())), precision=HIGHEST, preferred_element_type=jnp.float32
    )


def eliminated(rows, first):
    sub = lax.broadcasted_iota(jnp.int32, (STRIP, TILE), 0)
    cols = [
        jnp.broadcast_to(rows[:, first + j : first + j + 1], (STRIP, TILE)) for j in range(STRIP)
    ]
    left, right = rows[:, :TILE], rows[:, TILE:]
    pivots = jnp.zeros((STRIP, TILE), jnp.float32)
    for j in range(STRIP):
        pivot = jnp.broadcast_to(cols[j][j : j + 1, :], (STRIP, TILE))
        pivots = jnp.where(sub == j, pivot, pivots)
        if j == STRIP - 1:
            break
        factor = jnp.where(sub > j, cols[j], 0.0) * (1.0 / pivot)
        for k in range(j + 1, STRIP):
            cols[k] = cols[k] - factor * jnp.broadcast_to(cols[k][j : j + 1, :], (STRIP, TILE))
        left = left - factor * jnp.broadcast_to(left[j : j + 1, :], (STRIP, TILE))
        right = right - factor * jnp.broadcast_to(right[j : j + 1, :], (STRIP, TILE))
    scale = lax.rsqrt(pivots)
    return left * scale, right * scale


def inverse_factor_kernel(gram_ref, inv_ref, work_ref, tile_ref):
    size = gram_ref.shape[0]
    work_ref[...] = gram_ref[...]
    inv_ref[...] = jnp.zeros_like(inv_ref)
    eye = (
        lax.broadcasted_iota(jnp.int32, (TILE, TILE), 0)
        == lax.broadcasted_iota(jnp.int32, (TILE, TILE), 1)
    ).astype(jnp.float32)
    for k in range(size // TILE):
        lo, hi = k * TILE, (k + 1) * TILE
        tile_ref[:, :TILE] = work_ref[lo:hi, lo:hi]
        tile_ref[:, TILE:] = eye
        for top in range(0, TILE, STRIP):
            end = top + STRIP
            left, right = eliminated(tile_ref[top:end, :], top)
            tile_ref[top:end, TILE:] = right
            if end < TILE:
                both = jnp.concatenate([left, right], axis=1)
                tile_ref[end:, :] = tile_ref[end:, :] - contract(left, both, 0, 0)[end:, :]
        own = tile_ref[:, TILE:]
        if k:
            inv_ref[lo:hi, :lo] = contract(own, inv_ref[lo:hi, :lo], 1, 0)
        inv_ref[lo:hi, lo:hi] = own
        if hi < size:
            below = contract(work_ref[hi:, lo:hi], own, 1, 1)
            work_ref[hi:, hi:] = work_ref[hi:, hi:] - contract(below, below, 1, 1)
            inv_ref[hi:, :hi] = inv_ref[hi:, :hi] - contract(below, inv_ref[lo:hi, :hi], 1, 0)


def inverse_factor(gram):
    size = gram.shape[0]
    return pl.pallas_call(
        inverse_factor_kernel,
        out_shape=jax.ShapeDtypeStruct((size, size), jnp.float32),
        in_specs=[pl.BlockSpec(memory_space=pltpu.VMEM)],
        out_specs=pl.BlockSpec(memory_space=pltpu.VMEM),
        scratch_shapes=[
            pltpu.VMEM((size, size), jnp.float32),
            pltpu.VMEM((TILE, 2 * TILE), jnp.float32),
        ],
        compiler_params=pltpu.CompilerParams(vmem_limit_bytes=24 << 20),
        cost_estimate=pl.CostEstimate(
            flops=20_000_000_000, bytes_accessed=2 << 20, transcendentals=512
        ),
        name="inverse_factor",
    )(gram)


def swapped(parts, axes):
    return lax.all_to_all(parts, axes, 0, 0, tiled=True)


def sent_to_all(array, axes):
    size = math.prod(lax.axis_size(a) for a in (axes if isinstance(axes, tuple) else (axes,)))
    return swapped(jnp.broadcast_to(array[None], (size, *array.shape)), axes)


ROW = ("x", "z")
COL = ("y", "core")


def shards(mom_a, grad_a, basis_a, mom_b, grad_b, basis_b):
    nx, nz, ny, nc = (lax.axis_size(a) for a in ("x", "z", "y", "core"))
    ix, iz, iy, ic = (lax.axis_index(a) for a in ("x", "z", "y", "core"))
    nrow, ncol = nx * nz, ny * nc
    rows_a, cols_a = mom_a.shape
    rows_b, cols_b = mom_b.shape
    own = basis_a.shape[0]
    rank = own * nrow
    part_a = cols_a // nx

    with jax.named_scope("buffers"):
        buf_b = MU * mom_b + grad_b
        both = jnp.concatenate([MU * mom_a + grad_a, basis_a], axis=0)
        both = both.reshape(rows_a + own, nx, part_a).transpose(1, 0, 2)
    with jax.named_scope("relayout_a"):
        both = swapped(both, "x")
        buf_a = both[:, :rows_a].reshape(nx * rows_a, part_a)
        bas_a = both[:, rows_a:].reshape(nx * own, part_a)
    with jax.named_scope("gather_basis_b"):
        full_b = sent_to_all(basis_b, ROW).reshape(rank, cols_b)
    with jax.named_scope("gather_basis_a"):
        full_a = sent_to_all(bas_a, "z")
        full_a = full_a.reshape(nz, nx, own, part_a).transpose(1, 0, 2, 3).reshape(rank, part_a)

    with jax.named_scope("project"):
        proj_a = contract(buf_a, full_a, 1, 1)
        proj_b = contract(buf_b, full_b, 1, 1)
        some_a = proj_a.shape[0] // ncol
        some_b = proj_b.shape[0] // ncol
        mixed = jnp.concatenate(
            [proj_a.reshape(ncol, some_a, rank), proj_b.reshape(ncol, some_b, rank)], axis=1
        )
        mixed = jnp.sum(swapped(mixed, COL), axis=0)
        sum_a = jnp.sum(sent_to_all(mixed[:some_a], "x"), axis=0)
        mixed = sent_to_all(jnp.concatenate([sum_a, mixed[some_a:]], axis=0), COL)
        proj_a = mixed[:, :some_a].reshape(ncol * some_a, rank)
        proj_b = mixed[:, some_a:].reshape(ncol * some_b, rank)

    with jax.named_scope("gram"):
        mine = lax.dynamic_slice_in_dim(proj_a, ix * rows_a, rows_a, 0)
        mine = jnp.pad(mine, ((0, rows_b - rows_a), (0, 0)))
        chosen = jnp.where(ic == 0, mine, proj_b)
        band = rank // ny
        left = lax.dynamic_slice_in_dim(chosen, iy * band, band, 1)
        piece = contract(left, chosen, 0, 0)
        piece = jnp.sum(swapped(piece.reshape(nrow, band // nrow, rank), ROW), axis=0)
        piece = sent_to_all(piece, ROW).reshape(band, rank)
        gram = sent_to_all(piece, "y").reshape(rank, rank)

    with jax.named_scope("products"):
        w_a = contract(proj_a, buf_a, 0, 0)
        w_b = contract(proj_b, buf_b, 0, 0)
        w_a = lax.psum_scatter(w_a, "z", scatter_dimension=0, tiled=True)
        w_b = jnp.sum(swapped(w_b.reshape(nrow, own, cols_b), ROW), axis=0)
        w_a = sent_to_all(w_a, "z").reshape(rank, part_a)
        w_b = sent_to_all(w_b, ROW).reshape(rank, cols_b)

    with jax.named_scope("factor"):
        inv = inverse_factor(gram)
        invs = sent_to_all(inv, "core")
        inv_a, inv_b = invs[0], invs[1]

    with jax.named_scope("finish"):
        ortho_a = contract(proj_a, inv_a, 1, 1)
        ortho_b = contract(proj_b, inv_b, 1, 1)
        trans_a = contract(inv_a, w_a, 1, 0)
        trans_b = contract(inv_b, w_b, 1, 0)
        squares = jnp.stack([jnp.sum(trans_a * trans_a, axis=1), jnp.sum(trans_b * trans_b, axis=1)])
        squares = sent_to_all(squares, ("x", "y", "core")).reshape(nx, ncol, 2, rank)
        sq_a = jnp.sum(squares[:, :, 0], axis=(0, 1))
        sq_b = jnp.sum(lax.dynamic_index_in_dim(squares[:, :, 1], ix, 0, keepdims=False), axis=0)
        norms_a = jnp.sqrt(sq_a + EPS)[:, None]
        norms_b = jnp.sqrt(sq_b + EPS)[:, None]
        basis_new_a = trans_a / norms_a
        basis_new_b = trans_b / norms_b
        scale_a = math.sqrt(rows_a * nrow * cols_a * ncol / rank)
        scale_b = math.sqrt(rows_b * nrow * cols_b * ncol / rank)
        mom_new_a = buf_a - (1.0 - MU) * contract(ortho_a, trans_a, 1, 0)
        mom_new_b = buf_b - (1.0 - MU) * contract(ortho_b, trans_b, 1, 0)
        upd_a = contract(ortho_a, basis_new_a, 1, 0) * scale_a
        upd_b = contract(ortho_b, basis_new_b, 1, 0) * scale_b
        out_b = lax.dynamic_slice_in_dim(basis_new_b, (ix * nz + iz) * own, own, 0)

    with jax.named_scope("relayout_out"):
        shares = lax.dynamic_index_in_dim(
            basis_new_a.reshape(nx, nz, own, part_a), iz, 1, keepdims=False
        )
        late = jnp.concatenate(
            [
                mom_new_a.reshape(nx, rows_a, part_a),
                upd_a.reshape(nx, rows_a, part_a),
                shares,
            ],
            axis=1,
        )
        late = swapped(late, "x")
        late = late.transpose(1, 0, 2).reshape(2 * rows_a + own, cols_a)
    return (
        late[:rows_a],
        late[rows_a : 2 * rows_a].astype(jnp.bfloat16),
        late[2 * rows_a :],
        mom_new_b,
        upd_b.astype(jnp.bfloat16),
        out_b,
    )


def solution(mesh):
    fine = Mesh(mesh.devices.reshape(4, 8, 4, 2), ("x", "z", "y", "core"))
    spec = P(ROW, COL)
    return jax.shard_map(
        shards, mesh=fine, in_specs=(spec,) * 6, out_specs=(spec,) * 6, check_vma=False
    )
```

time: 717 us -> 307 us (0.43)
  other arithmetic: 254 us -> 3.53 us
  blocking collectives: 141 us -> 45.7 us
  waiting for transfers between devices: 198 us -> 117 us
  starting transfers between devices: 20.7 us -> 68.3 us
  matrix products: 42 us -> 19.1 us
  Pallas kernels: 0 us -> 22.5 us
  local copies, waits for them, and re-layouts: 35.4 us -> 14.1 us
    another operation x33 -> x1, other arithmetic: 246 us -> 0.01 us  [shards(): jnp.stack([jnp.sum(trans_a * trans_a, axis=1), jnp.sum(trans_b * trans_b,...]
    psum x1 -> x0, waiting for transfers between devices: 149 us -> none  [together(): so_far = lax.psum(jnp.concatenate([a.ravel() for a in arrays]), axis)]
    all_gather x2 -> x0, blocking collectives: 101 us -> none  [the longest x1 52.2 us: project(): lax.all_gather(basis, 'row', axis=0, tiled=True)]
    all_to_all x4 -> x12, waiting for transfers between devices: 24.8 us -> 117 us  [swapped(): return lax.all_to_all(parts, axes, 0, 0, tiled=True)]
    all_to_all x4 -> x12, starting transfers between devices: 20 us -> 68.3 us  [swapped(): return lax.all_to_all(parts, axes, 0, 0, tiled=True)]
    all_gather x2 -> x0, waiting for transfers between devices: 23.3 us -> none  [the longest x1 23.3 us: project(): lax.all_gather(basis, 'row', axis=0, tiled=True)]
    pallas_call x0 -> x1, Pallas kernels: none -> 22.5 us  [inverse_factor(): pl.pallas_call(inverse_factor_kernel, out_shape=jax.ShapeDtypeStruct((siz...]
    another operation x33 -> x0, local copies, waits for them, and re-layouts: 19 us -> none
  transfers between devices with their start and end apart: 7 -> 13, of which waited for: 4 -> 11; matrix products, arithmetic and copies ran while one was open for 25% -> 6% of each run, Pallas kernels for 0% -> 7%
where the time goes in v1:
time: 307 us; the launch traced here: 304 us
  waiting for transfers between devices  117 us (38%)
  starting transfers between devices  68.3 us (22%)
  blocking collectives  45.7 us (15%)
  Pallas kernels  22.5 us (7%)
  matrix products  19.1 us (6%)
  between operations  14.5 us (5%)
  local copies, waits for them, and re-layouts  14.1 us (5%)
  other arithmetic  3.53 us (1%)
    all_to_all x12, waiting for transfers between devices, swapped(): return lax.all_to_all(parts, axes, 0, 0, tiled=True)  117 us
    all_to_all x12, starting transfers between devices, swapped(): return lax.all_to_all(parts, axes, 0, 0, tiled=True)  68.3 us
    all_to_all x3, blocking collectives, swapped(): return lax.all_to_all(parts, axes, 0, 0, tiled=True)  45.7 us
    pallas_call x1, Pallas kernels, inverse_factor(): pl.pallas_call(inverse_factor_kernel, out_shape=jax.ShapeDtypeStruct((siz...  22.5 us
    dot_general x13, matrix products, contract(): lax.dot_general(a, b, (((ca,), (cb,)), ((), ())), precision=HIGHEST, pref...  19.1 us
    broadcast_in_dim x11, local copies, waits for them, and re-layouts, sent_to_all(): return swapped(jnp.broadcast_to(array[None], (size, *array.shape)), axes)  10.4 us
  transfers between devices with their start and end apart: 13, of which 11 were waited for; matrix products, arithmetic and copies ran while one was open for 6% of the time, Pallas kernels for 7%

profile of v1, /device:TPU:2, one launch (start us, length us, event | category | flops | bytes accessed | tf_op | source)
XLA Modules:
  0.0 304.5 jit_solution(8833082025036717247)
XLA Ops:
  9.2 11.2 %all_to_all.75 = f32[4,64,384]{2,1,0:T(8,128)S(1)} all-to-all(f32[4,64,384]{2,1,0:T(8,128)S(1)} %bitcast.103), channel_id=1, replica_groups=mesh['x'=4,'z'=8,'y'=4,'core'=2] {'x'}, dimensions={0} | all-to-all | bytes 786432 | tf_op jit(solution)/shard_map/relayout_a/all_to_all | solution.py:95
  21.3 10.7 %all-to-all-start.2 = ((f32[32,16,192]{2,1,0:T(8,128)}), f32[32,16,192]{2,1,0:T(8,128)S(1)}, u32[]{:S(2)}, u32[]{:S(2)}) async-start(f32[32,16,192]{2,1,0:T(8,128)} %broadcast_in_dim.26), calls=%async_computation.2 | async-start | bytes 1048576 | tf_op jit(solution)/shard_map/gather_basis_b/all_to_all | solution.py:95
  32.1 14.2 %all-to-all-done.2 = f32[32,16,192]{2,1,0:T(8,128)S(1)} async-done(((f32[32,16,192]{2,1,0:T(8,128)}), f32[32,16,192]{2,1,0:T(8,128)S(1)}, u32[]{:S(2)}, u32[]{:S(2)}) %all-to-all-start.2) | async-done | bytes 393248 | tf_op jit(solution)/shard_map/gather_basis_b/all_to_all | solution.py:95
  47.2 4.7 %all-to-all-start.1 = ((f32[8,64,384]{2,1,0:T(8,128)}), f32[8,64,384]{2,1,0:T(8,128)S(1)}, u32[]{:S(2)}, u32[]{:S(2)}) async-start(f32[8,64,384]{2,1,0:T(8,128)} %broadcast_in_dim.25), calls=%async_computation.1 | async-start | bytes 1572864 | tf_op jit(solution)/shard_map/gather_basis_a/all_to_all | solution.py:95
  52.8 19.8 %all-to-all-done.1 = f32[8,64,384]{2,1,0:T(8,128)S(1)} async-done(((f32[8,64,384]{2,1,0:T(8,128)}), f32[8,64,384]{2,1,0:T(8,128)S(1)}, u32[]{:S(2)}, u32[]{:S(2)}) %all-to-all-start.1) | async-done | bytes 786464 | tf_op jit(solution)/shard_map/gather_basis_a/all_to_all | solution.py:95
  73.7 18.9 %all_to_all.76 = f32[8,52,512]{2,1,0:T(8,128)S(1)} all-to-all(f32[8,52,512]{2,1,0:T(8,128)S(1)} %pad_maximum_fusion), channel_id=1, replica_groups=mesh['x'=4,'z'=8,'y'=4,'core'=2] {'y','core'}, dimensions={0} | all-to-all | bytes 1703936 | tf_op jit(solution)/shard_map/project/all_to_all | solution.py:95
  93.5 4.6 %all-to-all-start.4 = ((f32[4,24,512]{2,1,0:T(8,128)}), f32[4,24,512]{2,1,0:T(8,128)S(1)}, u32[]{:S(2)}, u32[]{:S(2)}) async-start(f32[4,24,512]{2,1,0:T(8,128)} %broadcast_in_dim.27), calls=%async_computation.4 | async-start | bytes 393216 | tf_op jit(solution)/shard_map/project/all_to_all | solution.py:95
  98.0 4.9 %all-to-all-done.4 = f32[4,24,512]{2,1,0:T(8,128)S(1)} async-done(((f32[4,24,512]{2,1,0:T(8,128)}), f32[4,24,512]{2,1,0:T(8,128)S(1)}, u32[]{:S(2)}, u32[]{:S(2)}) %all-to-all-start.4) | async-done | bytes 196640 | tf_op jit(solution)/shard_map/project/all_to_all | solution.py:95
  103.9 3.6 %all-to-all-start.5 = ((f32[8,52,512]{2,1,0:T(8,128)}), f32[8,52,512]{2,1,0:T(8,128)S(1)}, u32[]{:S(2)}, u32[]{:S(2)}) async-start(f32[8,52,512]{2,1,0:T(8,128)} %broadcast_in_dim.28), calls=%async_computation.5 | async-start | bytes 1835008 | tf_op jit(solution)/shard_map/project/all_to_all | solution.py:95
  107.5 14.5 %all-to-all-done.5 = f32[8,52,512]{2,1,0:T(8,128)S(1)} async-done(((f32[8,52,512]{2,1,0:T(8,128)}), f32[8,52,512]{2,1,0:T(8,128)S(1)}, u32[]{:S(2)}, u32[]{:S(2)}) %all-to-all-start.5) | async-done | bytes 852000 | tf_op jit(solution)/shard_map/project/all_to_all | solution.py:95
  122.7 15.6 %all_to_all.77 = f32[32,4,512]{2,1,0:T(4,128)S(1)} all-to-all(f32[32,4,512]{2,1,0:T(4,128)S(1)} %reshape.98), channel_id=1, replica_groups=mesh['x'=4,'z'=8,'y'=4,'core'=2] {'x','z'}, dimensions={0} | all-to-all | bytes 524288 | tf_op jit(solution)/shard_map/gram/all_to_all | solution.py:95
  139.1 5.7 %all-to-all-start.7 = ((f32[32,4,512]{2,1,0:T(4,128)}), f32[32,4,512]{2,1,0:T(4,128)S(1)}, u32[]{:S(2)}, u32[]{:S(2)}) async-start(f32[32,4,512]{2,1,0:T(4,128)} %broadcast_in_dim.29), calls=%async_computation.7 | async-start | bytes 524288 | tf_op jit(solution)/shard_map/gram/all_to_all | solution.py:95
  146.4 8.5 %all-to-all-done.7 = f32[32,4,512]{2,1,0:T(4,128)S(1)} async-done(((f32[32,4,512]{2,1,0:T(4,128)}), f32[32,4,512]{2,1,0:T(4,128)S(1)}, u32[]{:S(2)}, u32[]{:S(2)}) %all-to-all-start.7) | async-done | bytes 262176 | tf_op jit(solution)/shard_map/gram/all_to_all | solution.py:95
  154.9 5.6 %all-to-all-start.11 = ((f32[32,16,192]{2,1,0:T(8,128)}), f32[32,16,192]{2,1,0:T(8,128)S(1)}, u32[]{:S(2)}, u32[]{:S(2)}) async-start(f32[32,16,192]{2,1,0:T(8,128)} %fusion.7), calls=%async_computation.12 | async-start | bytes 1048576 | tf_op jit(solution)/shard_map/products/all_to_all | solution.py:95
  160.6 13.4 %all-to-all-done.11 = f32[32,16,192]{2,1,0:T(8,128)S(1)} async-done(((f32[32,16,192]{2,1,0:T(8,128)}), f32[32,16,192]{2,1,0:T(8,128)S(1)}, u32[]{:S(2)}, u32[]{:S(2)}) %all-to-all-start.11) | async-done | bytes 393248 | tf_op jit(solution)/shard_map/products/all_to_all | solution.py:95
  175.1 3.5 %all-to-all-start.8 = ((f32[4,128,512]{2,1,0:T(8,128)}), f32[4,128,512]{2,1,0:T(8,128)S(1)}, u32[]{:S(2)}, u32[]{:S(2)}) async-start(f32[4,128,512]{2,1,0:T(8,128)} %broadcast_in_dim.31), calls=%async_computation.8 | async-start | bytes 2097152 | tf_op jit(solution)/shard_map/gram/all_to_all | solution.py:95
  178.7 2.0 fusion.16
  180.7 8.7 %all-to-all-done.8 = f32[4,128,512]{2,1,0:T(8,128)S(1)} async-done(((f32[4,128,512]{2,1,0:T(8,128)}), f32[4,128,512]{2,1,0:T(8,128)S(1)}, u32[]{:S(2)}, u32[]{:S(2)}) %all-to-all-start.8) | async-done | bytes 1048608 | tf_op jit(solution)/shard_map/gram/all_to_all | solution.py:95
  190.3 9.2 %all-to-all-start.12 = ((f32[32,16,192]{2,1,0:T(8,128)}), f32[32,16,192]{2,1,0:T(8,128)}, u32[]{:S(2)}, u32[]{:S(2)}) async-start(f32[32,16,192]{2,1,0:T(8,128)} %broadcast_in_dim.34), calls=%async_computation.13 | async-start | bytes 1048576 | tf_op jit(solution)/shard_map/products/all_to_all | solution.py:95
  199.5 22.5 %inverse_factor.1 = f32[512,512]{1,0:T(8,128)S(1)} custom-call(f32[512,512]{1,0:T(8,128)S(1)} %bitcast.86), custom_call_target="tpu_custom_call" | custom-call | flops 20000000000 | bytes 2097152 | tf_op jit(solution)/shard_map/factor/inverse_factor/pallas_call | solution.py:77
  223.6 3.8 %all-to-all-start.9 = ((f32[2,512,512]{2,1,0:T(8,128)}), f32[2,512,512]{2,1,0:T(8,128)S(1)}, u32[]{:S(2)}, u32[]{:S(2)}) async-start(f32[2,512,512]{2,1,0:T(8,128)} %broadcast_in_dim.32), calls=%async_computation.9 | async-start | bytes 4194304 | tf_op jit(solution)/shard_map/factor/all_to_all | solution.py:95
  227.4 2.8 all-to-all-done.9
  230.3 1.8 broadcast_in_dim.33
  232.1 6.6 %all-to-all-start.10 = ((f32[8,64,384]{2,1,0:T(8,128)}), f32[8,64,384]{2,1,0:T(8,128)}, u32[]{:S(2)}, u32[]{:S(2)}) async-start(f32[8,64,384]{2,1,0:T(8,128)} %broadcast_in_dim.33), calls=%async_computation.11 | async-start | bytes 1572864 | tf_op jit(solution)/shard_map/products/all_to_all | solution.py:95
  239.9 2.5 multiply_reduce_fusion.1
  243.6 1.9 fusion.4
  245.5 16.7 %all-to-all-done.10 = f32[8,64,384]{2,1,0:T(8,128)} async-done(((f32[8,64,384]{2,1,0:T(8,128)}), f32[8,64,384]{2,1,0:T(8,128)}, u32[]{:S(2)}, u32[]{:S(2)}) %all-to-all-start.10) | async-done | bytes 786464 | tf_op jit(solution)/shard_map/products/all_to_all | solution.py:95
  262.3 3.0 multiply_reduce_fusion
  266.0 5.6 %all-to-all-start.13 = ((f32[32,2,512]{2,1,0:T(2,128)}), f32[32,2,512]{2,1,0:T(2,128)S(1)}, u32[]{:S(2)}, u32[]{:S(2)}) async-start(f32[32,2,512]{2,1,0:T(2,128)} %broadcast_in_dim.35), calls=%async_computation.14 | async-start | bytes 262144 | tf_op jit(solution)/shard_map/finish/all_to_all | solution.py:95
  273.4 4.8 %all-to-all-done.13 = f32[32,2,512]{2,1,0:T(2,128)S(1)} async-done(((f32[32,2,512]{2,1,0:T(2,128)}), f32[32,2,512]{2,1,0:T(2,128)S(1)}, u32[]{:S(2)}, u32[]{:S(2)}) %all-to-all-start.13) | async-done | bytes 131104 | tf_op jit(solution)/shard_map/finish/all_to_all | solution.py:95
  280.3 4.9 %all-to-all-start.14 = ((f32[4,112,384]{2,1,0:T(8,128)}), f32[4,112,384]{2,1,0:T(8,128)S(1)}, u32[]{:S(2)}, u32[]{:S(2)}) async-start(f32[4,112,384]{2,1,0:T(8,128)} %pad_maximum_fusion.1), calls=%async_computation.15 | async-start | bytes 1376256 | tf_op jit(solution)/shard_map/relayout_out/all_to_all | solution.py:95
  287.2 8.3 %all-to-all-done.14 = f32[4,112,384]{2,1,0:T(8,128)S(1)} async-done(((f32[4,112,384]{2,1,0:T(8,128)}), f32[4,112,384]{2,1,0:T(8,128)S(1)}, u32[]{:S(2)}, u32[]{:S(2)}) %all-to-all-start.14) | async-done | bytes 688160 | tf_op jit(solution)/shard_map/relayout_out/all_to_all | solution.py:95
  (86 shorter events, 25.6 us)
Async XLA Ops:
  7.2 13.3 %copy-start.9 = (f32[16,192]{1,0:T(8,128)S(1)}, f32[16,192]{1,0:T(8,128)}, u32[]{:S(2)}) copy-start(f32[16,192]{1,0:T(8,128)} %param.11) | copy-start | bytes 36868
  20.5 31.4 %copy-start.7 = (f32[224,192]{0,1:T(8,128)S(1)}, f32[224,192]{0,1:T(8,128)}, u32[]{:S(2)}) copy-start(f32[224,192]{0,1:T(8,128)} %param.10) | copy-start | bytes 516100
  20.5 31.4 %copy-start.8 = (f32[224,192]{0,1:T(8,128)S(1)}, f32[224,192]{0,1:T(8,128)}, u32[]{:S(2)}) copy-start(f32[224,192]{0,1:T(8,128)} %param.9) | copy-start | bytes 516100
  21.3 24.9 %all-to-all-start.2 = ((f32[32,16,192]{2,1,0:T(8,128)}), f32[32,16,192]{2,1,0:T(8,128)S(1)}, u32[]{:S(2)}, u32[]{:S(2)}) async-start(f32[32,16,192]{2,1,0:T(8,128)} %broadcast_in_dim.26), calls=%async_computation.2 | async-start | bytes 1048576 | tf_op jit(solution)/shard_map/gather_basis_b/all_to_all | solution.py:95
  47.2 25.4 %all-to-all-start.1 = ((f32[8,64,384]{2,1,0:T(8,128)}), f32[8,64,384]{2,1,0:T(8,128)S(1)}, u32[]{:S(2)}, u32[]{:S(2)}) async-start(f32[8,64,384]{2,1,0:T(8,128)} %broadcast_in_dim.25), calls=%async_computation.1 | async-start | bytes 1572864 | tf_op jit(solution)/shard_map/gather_basis_a/all_to_all | solution.py:95
  93.5 9.4 %all-to-all-start.4 = ((f32[4,24,512]{2,1,0:T(8,128)}), f32[4,24,512]{2,1,0:T(8,128)S(1)}, u32[]{:S(2)}, u32[]{:S(2)}) async-start(f32[4,24,512]{2,1,0:T(8,128)} %broadcast_in_dim.27), calls=%async_computation.4 | async-start | bytes 393216 | tf_op jit(solution)/shard_map/project/all_to_all | solution.py:95
  103.9 18.0 %all-to-all-start.5 = ((f32[8,52,512]{2,1,0:T(8,128)}), f32[8,52,512]{2,1,0:T(8,128)S(1)}, u32[]{:S(2)}, u32[]{:S(2)}) async-start(f32[8,52,512]{2,1,0:T(8,128)} %broadcast_in_dim.28), calls=%async_computation.5 | async-start | bytes 1835008 | tf_op jit(solution)/shard_map/project/all_to_all | solution.py:95
  122.1 56.5 %copy-start = (f32[8,24,512]{2,1,0:T(8,128)}, f32[8,24,512]{2,1,0:T(8,128)S(1)}, u32[]{:S(2)}) copy-start(f32[8,24,512]{2,1,0:T(8,128)S(1)} %slice.66) | copy-start | bytes 1179652
  139.1 15.8 %all-to-all-start.7 = ((f32[32,4,512]{2,1,0:T(4,128)}), f32[32,4,512]{2,1,0:T(4,128)S(1)}, u32[]{:S(2)}, u32[]{:S(2)}) async-start(f32[32,4,512]{2,1,0:T(4,128)} %broadcast_in_dim.29), calls=%async_computation.7 | async-start | bytes 524288 | tf_op jit(solution)/shard_map/gram/all_to_all | solution.py:95
  154.9 19.1 %all-to-all-start.11 = ((f32[32,16,192]{2,1,0:T(8,128)}), f32[32,16,192]{2,1,0:T(8,128)S(1)}, u32[]{:S(2)}, u32[]{:S(2)}) async-start(f32[32,16,192]{2,1,0:T(8,128)} %fusion.7), calls=%async_computation.12 | async-start | bytes 1048576 | tf_op jit(solution)/shard_map/products/all_to_all | solution.py:95
  175.1 14.4 %all-to-all-start.8 = ((f32[4,128,512]{2,1,0:T(8,128)}), f32[4,128,512]{2,1,0:T(8,128)S(1)}, u32[]{:S(2)}, u32[]{:S(2)}) async-start(f32[4,128,512]{2,1,0:T(8,128)} %broadcast_in_dim.31), calls=%async_computation.8 | async-start | bytes 2097152 | tf_op jit(solution)/shard_map/gram/all_to_all | solution.py:95
  178.6 48.8 %reduce-scatter.2.cloned.1.call-start = ((), (), s32[]{:S(2)}) async-start(), calls=%async_computation.16 | async-start | bytes 884736 | tf_op jit(solution)/shard_map/products/reduce_scatter | solution.py:159
  190.3 31.7 %all-to-all-start.12 = ((f32[32,16,192]{2,1,0:T(8,128)}), f32[32,16,192]{2,1,0:T(8,128)}, u32[]{:S(2)}, u32[]{:S(2)}) async-start(f32[32,16,192]{2,1,0:T(8,128)} %broadcast_in_dim.34), calls=%async_computation.13 | async-start | bytes 1048576 | tf_op jit(solution)/shard_map/products/all_to_all | solution.py:95
  223.6 6.6 %all-to-all-start.9 = ((f32[2,512,512]{2,1,0:T(8,128)}), f32[2,512,512]{2,1,0:T(8,128)S(1)}, u32[]{:S(2)}, u32[]{:S(2)}) async-start(f32[2,512,512]{2,1,0:T(8,128)} %broadcast_in_dim.32), calls=%async_computation.9 | async-start | bytes 4194304 | tf_op jit(solution)/shard_map/factor/all_to_all | solution.py:95
  232.1 30.2 %all-to-all-start.10 = ((f32[8,64,384]{2,1,0:T(8,128)}), f32[8,64,384]{2,1,0:T(8,128)}, u32[]{:S(2)}, u32[]{:S(2)}) async-start(f32[8,64,384]{2,1,0:T(8,128)} %broadcast_in_dim.33), calls=%async_computation.11 | async-start | bytes 1572864 | tf_op jit(solution)/shard_map/products/all_to_all | solution.py:95
  239.8 2.5 copy-start.2
  239.9 3.8 %copy-start.1 = (f32[8,24,512]{2,1,0:T(8,128)S(1)}, f32[8,24,512]{2,1,0:T(8,128)}, u32[]{:S(2)}) copy-start(f32[8,24,512]{2,1,0:T(8,128)} %copy-done) | copy-start | bytes 1179652
  242.3 19.9 %copy-start.5 = (f32[512,192]{0,1:T(8,128)}, f32[512,192]{0,1:T(8,128)S(1)}, u32[]{:S(2)}) copy-start(f32[512,192]{0,1:T(8,128)S(1)} %get-tuple-element.37) | copy-start | bytes 1179652
  265.3 13.2 %copy-start.4 = (f32[192,512]{1,0:T(8,128)S(1)}, f32[192,512]{1,0:T(8,128)}, u32[]{:S(2)}) copy-start(f32[192,512]{1,0:T(8,128)} %fusion.4) | copy-start | bytes 1179652
  266.0 12.2 %all-to-all-start.13 = ((f32[32,2,512]{2,1,0:T(2,128)}), f32[32,2,512]{2,1,0:T(2,128)S(1)}, u32[]{:S(2)}, u32[]{:S(2)}) async-start(f32[32,2,512]{2,1,0:T(2,128)} %broadcast_in_dim.35), calls=%async_computation.14 | async-start | bytes 262144 | tf_op jit(solution)/shard_map/finish/all_to_all | solution.py:95
  278.5 6.7 %copy-start.6 = (f32[512,192]{0,1:T(8,128)S(1)}, f32[512,192]{0,1:T(8,128)}, u32[]{:S(2)}) copy-start(f32[512,192]{0,1:T(8,128)} %copy-done.5) | copy-start | bytes 1179652
  279.3 6.7 %copy-start.3 = (f32[224,512]{1,0:T(8,128)S(1)}, f32[224,512]{1,0:T(8,128)}, u32[]{:S(2)}) copy-start(f32[224,512]{1,0:T(8,128)} %copy-done.2) | copy-start | bytes 1376260
  280.3 15.2 %all-to-all-start.14 = ((f32[4,112,384]{2,1,0:T(8,128)}), f32[4,112,384]{2,1,0:T(8,128)S(1)}, u32[]{:S(2)}, u32[]{:S(2)}) async-start(f32[4,112,384]{2,1,0:T(8,128)} %pad_maximum_fusion.1), calls=%async_computation.15 | async-start | bytes 1376256 | tf_op jit(solution)/shard_map/relayout_out/all_to_all | solution.py:95
Sparse Core Ops, SparseCore 0:
  182.0 40.0 reduce-scatter.1
